TPU v7x, 256 devices: a whole 4x4x8 slice. The times are simulated.
256 devices in a mesh: segment: 4 (over x), shard: 64 (over y, z, core).
Axes of the slice: x: 4, y: 4, z: 8, core: 2. Of those that a mesh axis runs over, the one named last changes fastest.
Arguments:
- tokens: bfloat16 [3, 128, 3072], P(None, 'shard'), may hold values from -6 to 6
- norm_gain: float32 [4, 3072], P('segment'), may hold values from 0.5 to 1.5
- w_gate: bfloat16 [4, 3072, 32768], P('segment', None, 'shard'), may hold values from -0.109375 to 0.109375
- w_up: bfloat16 [4, 3072, 32768], P('segment', None, 'shard'), may hold values from -0.109375 to 0.109375
- w_down: bfloat16 [4, 32768, 3072], P('segment', 'shard'), may hold values from -0.046875 to 0.046875
- block_counts: int32 [4], P('segment'), may hold values from 1 to 2
- gate_prob: float32 [4, 3, 128], P('segment', None, 'shard'), may hold values from 0.1 to 1
Outputs:
- section_outputs: bfloat16 [4, 3, 128, 3072], P('segment', None, 'shard')
All inputs are finite; a program needn't handle non-finite values.
Results may differ from a plain program's by a relative error of at most 0.009.
Values may be sent and summed in bfloat16 or wider, within the bound.
A program may use at most 64 MiB of HBM per device.

v0:
```python
import jax
import jax.numpy as jnp
from jax import lax
from jax.sharding import PartitionSpec as P

FF = 16384


def shifted(value, axis, steps):
    count = lax.axis_size(axis)
    initial, last = (max(0, -steps), min(count, count - steps))
    return lax.ppermute(value, axis, [(source, source + steps) for source in range(initial, last)])


def normalize(rows, row_gain):
    values = rows.astype(jnp.float32)
    scale = lax.rsqrt(jnp.mean(values * values, axis=-1, keepdims=True) + 1e-05)
    return (values * scale * row_gain).astype(jnp.bfloat16)


def expert_rows(normed, gate_part, up_part, down_part):
    gate_val = jnp.dot(normed, gate_part, preferred_element_type=jnp.float32)
    up_val = jnp.dot(normed, up_part, preferred_element_type=jnp.float32)
    hidden = (jax.nn.silu(gate_val) * up_val).astype(jnp.bfloat16)
    return jnp.dot(hidden, down_part, preferred_element_type=jnp.float32)


def shards(tokens, norm_gain, w_gate, w_up, w_down, block_counts, gate_prob):
    segment_index = lax.axis_index("segment")
    segment_count = lax.axis_size("segment")
    shard_count = lax.axis_size("shard")
    hidden_count = w_gate.shape[2]
    own_expert = lax.axis_index("shard") // (FF // hidden_count)
    zero_blocks = block_counts[0]
    row_gain = norm_gain[0]
    gate_part = w_gate[0]
    up_part = w_up[0]
    down_part = w_down[0]
    probs = gate_prob[0]
    block_total = tokens.shape[0]
    local_rows = tokens.shape[1]
    width = tokens.shape[2]
    first_block = jnp.where(own_expert == 0, 0, zero_blocks)
    last_block = jnp.where(own_expert == 0, zero_blocks, block_total)
    carried = tokens
    stored = jnp.zeros_like(tokens)
    for tick in range(segment_count):
        normed = normalize(carried, row_gain)
        gathered = lax.all_gather(normed, "shard", axis=1, tiled=True)
        partial_sum = jnp.zeros(gathered.shape, jnp.float32)

        def add_block(block_id, acc):
            block_rows = lax.dynamic_index_in_dim(gathered, block_id, 0, keepdims=False)
            result = expert_rows(block_rows, gate_part, up_part, down_part)
            return lax.dynamic_update_index_in_dim(acc, result, block_id, 0)

        partial_sum = lax.fori_loop(first_block, last_block, add_block, partial_sum)
        split_terms = partial_sum.reshape(block_total, shard_count, local_rows, width)
        received = lax.all_to_all(split_terms, "shard", split_axis=1, concat_axis=1, tiled=True)
        mixed = jnp.sum(received, axis=1)
        updated = (carried.astype(jnp.float32) + probs[:, :, None] * mixed).astype(jnp.bfloat16)
        stored = jnp.where(segment_index == tick, updated, stored)
        if tick + 1 < segment_count:
            carried = shifted(updated, "segment", 1)
    return stored[None]


def solution(mesh):
    placed = (
        P(None, "shard", None),
        P("segment", None),
        P("segment", None, "shard"),
        P("segment", None, "shard"),
        P("segment", "shard", None),
        P("segment"),
        P("segment", None, "shard"),
    )
    return jax.shard_map(
        shards,
        mesh=mesh,
        in_specs=placed,
        out_specs=P("segment", None, "shard", None),
        check_vma=False,
    )
```

profile of v0, /device:TPU:5, one launch (start us, length us, event | category | flops | bytes accessed | tf_op | source)
XLA Modules:
  0.0 946.9 jit_solution(11908347532508689451)
XLA Ops:
  6.5 0.9 fusion.76
  7.4 0.9 fusion.78
  8.3 0.6 copy.26
  9.6 82.2 %all-gather.5.cloned.1.call-done = bf16[3,128,3072]{2,0,1:T(4,128)(2,1)} async-done(((bf16[3,2,3072]{2,0,1:T(4,128)(2,1)}), bf16[3,128,3072]{2,0,1:T(4,128)(2,1)}) %all-gather.5.cloned.1.call-update) | async-done | bytes 2359312 | tf_op jit(solution)/shard_map/all_gather | solution.py:49
  91.9 4.2 copy.27
  96.1 2.7 broadcast.59.clone
  98.9 7.1 while.40
  98.9 1.7 fusion.138
  100.6 5.4 fusion.139
  106.0 6.6 reshape.46
  112.6 6.1 copy.28
  118.6 13.8 %all-to-all-start = ((f32[3,64,2,3072]{3,2,0,1:T(2,128)}), f32[3,64,2,3072]{3,2,0,1:T(2,128)}, u32[]{:S(2)}, u32[]{:S(2)}) async-start(f32[3,64,2,3072]{3,2,0,1:T(2,128)} %copy.28), calls=%async_computation | async-start | bytes 9437184 | tf_op jit(solution)/shard_map/all_to_all | solution.py:59
  132.6 107.0 %all-to-all-done = f32[3,64,2,3072]{3,2,0,1:T(2,128)} async-done(((f32[3,64,2,3072]{3,2,0,1:T(2,128)}), f32[3,64,2,3072]{3,2,0,1:T(2,128)}, u32[]{:S(2)}, u32[]{:S(2)}) %all-to-all-start) | async-done | bytes 4718624 | tf_op jit(solution)/shard_map/all_to_all | solution.py:59
  239.6 3.7 reduce_sum.73
  243.2 0.1 fusion.79
  243.3 2.8 collective-permute-start
  246.2 1.9 collective-permute-done
  248.1 0.1 fusion.80
  248.2 0.1 fusion.82
  248.3 0.6 copy.29
  249.0 76.5 %all-gather.7.cloned.1.call-done = bf16[3,128,3072]{2,0,1:T(4,128)(2,1)} async-done(((bf16[3,2,3072]{2,0,1:T(4,128)(2,1)}), bf16[3,128,3072]{2,0,1:T(4,128)(2,1)}) %all-gather.7.cloned.1.call-update) | async-done | bytes 2359312 | tf_op jit(solution)/shard_map/all_gather | solution.py:49
  325.5 4.2 copy.30
  329.7 2.7 broadcast.59.clone.1
  332.4 7.1 while.41
  332.4 1.7 fusion.145
  334.2 5.4 fusion.146
  339.5 6.6 reshape.47
  346.1 4.0 copy.31
  350.1 120.6 %all_to_all.20 = f32[3,64,2,3072]{3,2,0,1:T(2,128)} all-to-all(f32[3,64,2,3072]{3,2,0,1:T(2,128)S(1)} %copy.31), channel_id=1, replica_groups=mesh['segment'=4,'shard'=64] {'shard'}, dimensions={1} | all-to-all | bytes 9437184 | tf_op jit(solution)/shard_map/all_to_all | solution.py:59
  470.6 3.7 reduce_sum.75
  474.3 0.1 fusion.83
  474.4 2.8 collective-permute-start.1
  477.2 1.9 collective-permute-done.1
  479.1 0.1 fusion.84
  479.3 0.1 fusion.86
  479.4 0.6 copy.32
  480.1 76.9 %all-gather.9.cloned.1.call-done = bf16[3,128,3072]{2,0,1:T(4,128)(2,1)} async-done(((bf16[3,2,3072]{2,0,1:T(4,128)(2,1)}), bf16[3,128,3072]{2,0,1:T(4,128)(2,1)}) %all-gather.9.cloned.1.call-update) | async-done | bytes 2359312 | tf_op jit(solution)/shard_map/all_gather | solution.py:49
  557.0 4.2 copy.33
  561.2 2.7 broadcast.59.clone.2
  563.9 7.1 while.42
  563.9 1.7 fusion.152
  565.6 5.4 fusion.153
  571.0 6.6 reshape.48
  577.6 4.0 copy.34
  581.6 120.6 %all_to_all.21 = f32[3,64,2,3072]{3,2,0,1:T(2,128)} all-to-all(f32[3,64,2,3072]{3,2,0,1:T(2,128)S(1)} %copy.34), channel_id=1, replica_groups=mesh['segment'=4,'shard'=64] {'shard'}, dimensions={1} | all-to-all | bytes 9437184 | tf_op jit(solution)/shard_map/all_to_all | solution.py:59
  702.1 3.7 reduce_sum.77
  705.8 0.1 fusion.87
  705.9 2.8 collective-permute-start.2
  708.7 1.9 collective-permute-done.2
  710.6 0.1 fusion.88
  710.8 0.1 fusion.90
  710.9 0.6 copy.35
  711.5 77.0 %all-gather.11.cloned.1.call-done = bf16[3,128,3072]{2,0,1:T(4,128)(2,1)} async-done(((bf16[3,2,3072]{2,0,1:T(4,128)(2,1)}), bf16[3,128,3072]{2,0,1:T(4,128)(2,1)}) %all-gather.11.cloned.1.call-update) | async-done | bytes 2359312 | tf_op jit(solution)/shard_map/all_gather | solution.py:49
  788.5 4.2 copy.36
  792.7 2.7 broadcast.59
  795.4 7.1 while.43
  795.4 1.7 fusion.159
  797.2 5.4 fusion.160
  802.5 6.6 reshape.49
  809.1 6.1 copy.37
  815.2 13.7 %all-to-all-start.3 = ((f32[3,64,2,3072]{3,2,0,1:T(2,128)}), f32[3,64,2,3072]{3,2,0,1:T(2,128)}, u32[]{:S(2)}, u32[]{:S(2)}) async-start(f32[3,64,2,3072]{3,2,0,1:T(2,128)} %copy.37), calls=%async_computation.3 | async-start | bytes 9437184 | tf_op jit(solution)/shard_map/all_to_all | solution.py:59
  828.9 107.1 %all-to-all-done.3 = f32[3,64,2,3072]{3,2,0,1:T(2,128)} async-done(((f32[3,64,2,3072]{3,2,0,1:T(2,128)}), f32[3,64,2,3072]{3,2,0,1:T(2,128)}, u32[]{:S(2)}, u32[]{:S(2)}) %all-to-all-start.3) | async-done | bytes 4718624 | tf_op jit(solution)/shard_map/all_to_all | solution.py:59
  936.0 3.7 reduce_sum.79
  939.7 0.7 fusion.92
  (25 shorter events, 0.4 us)
Async XLA Ops:
  6.5 85.3 %all-gather.5.cloned.1.call-start = ((), (), s32[]{:S(2)}) async-start(), calls=%async_computation.4 | async-start | bytes 3194880 | tf_op jit(solution)/shard_map/all_gather | solution.py:49
  96.1 2.8 copy-start
  118.6 13.9 %copy-start.5 = (f32[1,3,2]{1,2,0:T(2,128)S(1)}, f32[1,3,2]{1,2,0:T(2,128)}, u32[]{:S(2)}) copy-start(f32[1,3,2]{1,2,0:T(2,128)} %param.21) | copy-start | bytes 76
  118.6 120.9 %all-to-all-start = ((f32[3,64,2,3072]{3,2,0,1:T(2,128)}), f32[3,64,2,3072]{3,2,0,1:T(2,128)}, u32[]{:S(2)}, u32[]{:S(2)}) async-start(f32[3,64,2,3072]{3,2,0,1:T(2,128)} %copy.28), calls=%async_computation | async-start | bytes 9437184 | tf_op jit(solution)/shard_map/all_to_all | solution.py:59
  132.4 110.8 %copy-start.1 = (bf16[3,2,3072]{2,1,0:T(2,128)(2,1)S(1)}, bf16[3,2,3072]{2,1,0:T(2,128)(2,1)}, u32[]{:S(2)}) copy-start(bf16[3,2,3072]{2,1,0:T(2,128)(2,1)} %param.15) | copy-start | bytes 110596
  132.4 115.8 %copy-start.2 = (f32[1,3072]{1,0:T(1,128)S(1)}, f32[1,3072]{1,0:T(1,128)}, u32[]{:S(2)}) copy-start(f32[1,3072]{1,0:T(1,128)} %param.16) | copy-start | bytes 36868
  132.4 193.1 %all-gather.7.cloned.1.call-start = ((), (), s32[]{:S(2)}) async-start(), calls=%async_computation.5 | async-start | bytes 3194880 | tf_op jit(solution)/shard_map/all_gather | solution.py:49
  243.3 4.7 collective-permute-start
  249.0 308.0 %all-gather.9.cloned.1.call-start = ((), (), s32[]{:S(2)}) async-start(), calls=%async_computation.6 | async-start | bytes 3194880 | tf_op jit(solution)/shard_map/all_gather | solution.py:49
  474.4 4.7 collective-permute-start.1
  480.0 308.5 %all-gather.11.cloned.1.call-start = ((), (), s32[]{:S(2)}) async-start(), calls=%async_computation.7 | async-start | bytes 3194880 | tf_op jit(solution)/shard_map/all_gather | solution.py:49
  705.9 89.5 %copy-start.3 = (bf16[3,2,3072]{2,1,0:T(2,128)(2,1)}, bf16[3,2,3072]{2,1,0:T(2,128)(2,1)S(1)}, u32[]{:S(2)}) copy-start(bf16[3,2,3072]{2,1,0:T(2,128)(2,1)S(1)} %fusion.87) | copy-start | bytes 110596
  705.9 4.7 collective-permute-start.2
  815.2 120.8 %all-to-all-start.3 = ((f32[3,64,2,3072]{3,2,0,1:T(2,128)}), f32[3,64,2,3072]{3,2,0,1:T(2,128)}, u32[]{:S(2)}, u32[]{:S(2)}) async-start(f32[3,64,2,3072]{3,2,0,1:T(2,128)} %copy.37), calls=%async_computation.3 | async-start | bytes 9437184 | tf_op jit(solution)/shard_map/all_to_all | solution.py:59
  828.8 110.8 %copy-start.4 = (bf16[3,2,3072]{2,1,0:T(2,128)(2,1)S(1)}, bf16[3,2,3072]{2,1,0:T(2,128)(2,1)}, u32[]{:S(2)}) copy-start(bf16[3,2,3072]{2,1,0:T(2,128)(2,1)} %copy-done.3) | copy-start | bytes 110596
Sparse Core Ops, SparseCore 0:
  10.1 81.7 all-gather.4
  249.1 76.3 all-gather.6
  480.1 76.8 all-gather.8
  711.6 76.8 all-gather.10
where the time goes:
time: 949 us; the launch traced here: 947 us
  waiting for transfers between devices  532 us (56%)
  blocking collectives  241 us (25%)
  local copies, waits for them, and re-layouts  76.8 us (8%)
  starting transfers between devices  36 us (4%)
  matrix products  28.3 us (3%)
  other arithmetic  18.2 us (2%)
  between operations  14 us (1%)
    all_gather x4, waiting for transfers between devices, shards(): gathered = lax.all_gather(normed, 'shard', axis=1, tiled=True)  313 us
    all_to_all x2, blocking collectives, shards(): lax.all_to_all(split_terms, 'shard', split_axis=1, concat_axis=1, tiled=T...  241 us
    all_to_all x2, waiting for transfers between devices, shards(): lax.all_to_all(split_terms, 'shard', split_axis=1, concat_axis=1, tiled=T...  214 us
    reshape x8, local copies, waits for them, and re-layouts, shards(): partial_sum.reshape(block_total, shard_count, local_rows, width)  46.4 us
    all_to_all x2, starting transfers between devices, shards(): lax.all_to_all(split_terms, 'shard', split_axis=1, concat_axis=1, tiled=T...  27.4 us
    dot_general x4, matrix products, expert_rows(): return jnp.dot(hidden, down_part, preferred_element_type=jnp.float32)  21.5 us
  transfers between devices with their start and end apart: 9, of which 9 were waited for; matrix products, arithmetic and copies ran while one was open for 0% of the time, Pallas kernels for 0%

commit v1 on v0

--- a/solution.py
+++ b/solution.py
@@ -46,7 +46,9 @@
     stored = jnp.zeros_like(tokens)
     for tick in range(segment_count):
         normed = normalize(carried, row_gain)
-        gathered = lax.all_gather(normed, "shard", axis=1, tiled=True)
+        gathered = jnp.concatenate(
+            lax.all_to_all(jnp.stack([normed] * lax.axis_size("shard")), "shard", 0, 0), axis=1
+        )
         partial_sum = jnp.zeros(gathered.shape, jnp.float32)
 
         def add_block(block_id, acc):

time: 949 us -> 920 us (0.969)
  waiting for transfers between devices: 532 us -> 389 us
  blocking collectives: 241 us -> 305 us
  local copies, waits for them, and re-layouts: 76.8 us -> 106 us
  starting transfers between devices: 36 us -> 62.5 us
  between operations: 14 us -> 1.09 us
    all_gather x4 -> x0, waiting for transfers between devices: 313 us -> none  [shards(): gathered = lax.all_gather(normed, 'shard', axis=1, tiled=True)]
    all_to_all x0 -> x3, waiting for transfers between devices: none -> 169 us  [shards(): lax.all_to_all(jnp.stack([normed] * lax.axis_size('shard')), 'shard', 0, 0)]
    all_to_all x0 -> x1, blocking collectives: none -> 64.2 us  [shards(): lax.all_to_all(jnp.stack([normed] * lax.axis_size('shard')), 'shard', 0, 0)]
    reshape x0 -> x8, local copies, waits for them, and re-layouts: none -> 39.5 us  [shards(): jnp.concatenate(lax.all_to_all(jnp.stack([normed] * lax.axis_size('shard'...]
    all_to_all x0 -> x3, starting transfers between devices: none -> 27.1 us  [shards(): lax.all_to_all(jnp.stack([normed] * lax.axis_size('shard')), 'shard', 0, 0)]
    while x4 -> x0, local copies, waits for them, and re-layouts: 16.9 us -> none  [shards(): partial_sum = lax.fori_loop(first_block, last_block, add_block, partial_sum)]
    another operation x4 -> x8, local copies, waits for them, and re-layouts: 10.8 us -> 19.8 us
  transfers between devices with their start and end apart: 9 -> 8, of which waited for: 9 -> 8; matrix products, arithmetic and copies ran while one was open for 0% -> 0% of each run, Pallas kernels for 0% -> 0%
where the time goes in v1:
time: 920 us; the launch traced here: 910 us
  waiting for transfers between devices  389 us (42%)
  blocking collectives  305 us (33%)
  local copies, waits for them, and re-layouts  106 us (12%)
  starting transfers between devices  62.5 us (7%)
  matrix products  28.3 us (3%)
  other arithmetic  18.2 us (2%)
    all_to_all x2, blocking collectives, shards(): lax.all_to_all(split_terms, 'shard', split_axis=1, concat_axis=1, tiled=T...  241 us
    all_to_all x2, waiting for transfers between devices, shards(): lax.all_to_all(split_terms, 'shard', split_axis=1, concat_axis=1, tiled=T...  214 us
    all_to_all x3, waiting for transfers between devices, shards(): lax.all_to_all(jnp.stack([normed] * lax.axis_size('shard')), 'shard', 0, 0)  169 us
    all_to_all x1, blocking collectives, shards(): lax.all_to_all(jnp.stack([normed] * lax.axis_size('shard')), 'shard', 0, 0)  64.2 us
    reshape x8, local copies, waits for them, and re-layouts, shards(): partial_sum.reshape(block_total, shard_count, local_rows, width)  46.5 us
    reshape x8, local copies, waits for them, and re-layouts, shards(): jnp.concatenate(lax.all_to_all(jnp.stack([normed] * lax.axis_size('shard'...  39.5 us
    all_to_all x3, starting transfers between devices, shards(): lax.all_to_all(jnp.stack([normed] * lax.axis_size('shard')), 'shard', 0, 0)  27.1 us
    all_to_all x2, starting transfers between devices, shards(): lax.all_to_all(split_terms, 'shard', split_axis=1, concat_axis=1, tiled=T...  26.9 us
  transfers between devices with their start and end apart: 8, of which 8 were waited for; matrix products, arithmetic and copies ran while one was open for 0% of the time, Pallas kernels for 0%

profile of v1, /device:TPU:5, one launch (start us, length us, event | category | flops | bytes accessed | tf_op | source)
XLA Modules:
  0.0 909.9 jit_solution(18052100580221268120)
XLA Ops:
  0.0 0.9 fusion.76
  0.9 0.9 fusion.78
  1.8 2.6 stack.8
  4.4 12.3 %all-to-all-start = ((bf16[64,3,2,3072]{3,2,1,0:T(2,128)(2,1)}), bf16[64,3,2,3072]{3,2,1,0:T(2,128)(2,1)S(1)}, u32[]{:S(2)}, u32[]{:S(2)}) async-start(bf16[64,3,2,3072]{3,2,1,0:T(2,128)(2,1)} %stack.8), calls=%async_computation | async-start | bytes 4718592 | tf_op jit(solution)/shard_map/all_to_all | solution.py:50
  17.4 56.0 %all-to-all-done = bf16[64,3,2,3072]{3,2,1,0:T(2,128)(2,1)S(1)} async-done(((bf16[64,3,2,3072]{3,2,1,0:T(2,128)(2,1)}), bf16[64,3,2,3072]{3,2,1,0:T(2,128)(2,1)S(1)}, u32[]{:S(2)}, u32[]{:S(2)}) %all-to-all-start) | async-done | bytes 2359328 | tf_op jit(solution)/shard_map/all_to_all | solution.py:50
  73.4 3.0 copy.11
  76.4 6.0 reshape.79
  82.4 2.7 broadcast.67.clone
  85.2 7.1 while.40
  85.2 1.7 fusion.138
  87.0 5.4 fusion.139
  92.3 6.6 reshape.80
  98.9 6.1 copy.12
  105.0 13.7 %all-to-all-start.1 = ((f32[3,64,2,3072]{3,2,0,1:T(2,128)}), f32[3,64,2,3072]{3,2,0,1:T(2,128)}, u32[]{:S(2)}, u32[]{:S(2)}) async-start(f32[3,64,2,3072]{3,2,0,1:T(2,128)} %copy.12), calls=%async_computation.1 | async-start | bytes 9437184 | tf_op jit(solution)/shard_map/all_to_all | solution.py:61
  118.8 106.8 %all-to-all-done.1 = f32[3,64,2,3072]{3,2,0,1:T(2,128)} async-done(((f32[3,64,2,3072]{3,2,0,1:T(2,128)}), f32[3,64,2,3072]{3,2,0,1:T(2,128)}, u32[]{:S(2)}, u32[]{:S(2)}) %all-to-all-start.1) | async-done | bytes 4718624 | tf_op jit(solution)/shard_map/all_to_all | solution.py:61
  225.7 3.7 reduce_sum.73
  229.4 2.8 collective-permute-start
  232.3 1.9 collective-permute-done
  234.1 0.1 fusion.80
  234.4 2.6 stack.9
  237.0 7.2 all-to-all-start.2
  244.2 56.6 %all-to-all-done.2 = bf16[64,3,2,3072]{3,2,1,0:T(2,128)(2,1)} async-done(((bf16[64,3,2,3072]{3,2,1,0:T(2,128)(2,1)}), bf16[64,3,2,3072]{3,2,1,0:T(2,128)(2,1)}, u32[]{:S(2)}, u32[]{:S(2)}) %all-to-all-start.2) | async-done | bytes 2359328 | tf_op jit(solution)/shard_map/all_to_all | solution.py:50
  300.8 4.7 copy.13
  305.4 6.0 reshape.82
  311.5 2.7 broadcast.67.clone.1
  314.1 7.1 while.41
  314.1 1.7 fusion.145
  315.9 5.4 fusion.146
  321.2 6.6 reshape.83
  327.8 4.0 copy.14
  331.8 120.2 %all_to_all.41 = f32[3,64,2,3072]{3,2,0,1:T(2,128)} all-to-all(f32[3,64,2,3072]{3,2,0,1:T(2,128)S(1)} %copy.14), channel_id=1, replica_groups=mesh['segment'=4,'shard'=64] {'shard'}, dimensions={1} | all-to-all | bytes 9437184 | tf_op jit(solution)/shard_map/all_to_all | solution.py:61
  451.9 3.7 reduce_sum.75
  455.7 2.8 collective-permute-start.1
  458.6 1.9 collective-permute-done.1
  460.4 0.1 fusion.84
  460.7 2.6 stack.10
  463.3 7.6 all-to-all-start.4
  470.9 56.6 %all-to-all-done.4 = bf16[64,3,2,3072]{3,2,1,0:T(2,128)(2,1)} async-done(((bf16[64,3,2,3072]{3,2,1,0:T(2,128)(2,1)}), bf16[64,3,2,3072]{3,2,1,0:T(2,128)(2,1)}, u32[]{:S(2)}, u32[]{:S(2)}) %all-to-all-start.4) | async-done | bytes 2359328 | tf_op jit(solution)/shard_map/all_to_all | solution.py:50
  527.5 4.7 copy.15
  532.1 6.0 reshape.85
  538.2 2.7 broadcast.67.clone.2
  540.9 7.1 while.42
  540.9 1.7 fusion.152
  542.6 5.4 fusion.153
  547.9 6.6 reshape.86
  554.5 4.0 copy.16
  558.5 120.6 %all_to_all.42 = f32[3,64,2,3072]{3,2,0,1:T(2,128)} all-to-all(f32[3,64,2,3072]{3,2,0,1:T(2,128)S(1)} %copy.16), channel_id=1, replica_groups=mesh['segment'=4,'shard'=64] {'shard'}, dimensions={1} | all-to-all | bytes 9437184 | tf_op jit(solution)/shard_map/all_to_all | solution.py:61
  679.1 3.7 reduce_sum.77
  682.8 2.8 collective-permute-start.2
  685.7 1.9 collective-permute-done.2
  687.8 1.2 stack.11
  689.0 64.2 %all_to_all.40 = bf16[64,3,2,3072]{3,2,1,0:T(2,128)(2,1)S(1)} all-to-all(bf16[64,3,2,3072]{3,2,1,0:T(2,128)(2,1)S(1)} %stack.11), channel_id=1, replica_groups=mesh['segment'=4,'shard'=64] {'shard'}, dimensions={0} | all-to-all | bytes 4718592 | tf_op jit(solution)/shard_map/all_to_all | solution.py:50
  753.2 3.0 copy.17
  756.2 6.0 reshape.88
  762.2 2.7 broadcast.67
  764.9 7.2 while.43
  764.9 1.7 fusion.159
  766.7 5.4 fusion.160
  772.2 6.6 reshape.89
  778.8 6.1 copy.18
  784.9 13.3 %all-to-all-start.7 = ((f32[3,64,2,3072]{3,2,0,1:T(2,128)}), f32[3,64,2,3072]{3,2,0,1:T(2,128)}, u32[]{:S(2)}, u32[]{:S(2)}) async-start(f32[3,64,2,3072]{3,2,0,1:T(2,128)} %copy.18), calls=%async_computation.7 | async-start | bytes 9437184 | tf_op jit(solution)/shard_map/all_to_all | solution.py:61
  798.2 107.1 %all-to-all-done.7 = f32[3,64,2,3072]{3,2,0,1:T(2,128)} async-done(((f32[3,64,2,3072]{3,2,0,1:T(2,128)}), f32[3,64,2,3072]{3,2,0,1:T(2,128)}, u32[]{:S(2)}, u32[]{:S(2)}) %all-to-all-start.7) | async-done | bytes 4718624 | tf_op jit(solution)/shard_map/all_to_all | solution.py:61
  905.3 3.7 reduce_sum.79
  908.9 0.7 fusion.92
  (24 shorter events, 1.0 us)
Async XLA Ops:
  4.4 69.0 %all-to-all-start = ((bf16[64,3,2,3072]{3,2,1,0:T(2,128)(2,1)}), bf16[64,3,2,3072]{3,2,1,0:T(2,128)(2,1)S(1)}, u32[]{:S(2)}, u32[]{:S(2)}) async-start(bf16[64,3,2,3072]{3,2,1,0:T(2,128)(2,1)} %stack.8), calls=%async_computation | async-start | bytes 4718592 | tf_op jit(solution)/shard_map/all_to_all | solution.py:50
  82.4 2.8 copy-start
  105.0 13.7 %copy-start.5 = (f32[1,3,2]{1,2,0:T(2,128)S(1)}, f32[1,3,2]{1,2,0:T(2,128)}, u32[]{:S(2)}) copy-start(f32[1,3,2]{1,2,0:T(2,128)} %param.21) | copy-start | bytes 76
  105.0 120.7 %all-to-all-start.1 = ((f32[3,64,2,3072]{3,2,0,1:T(2,128)}), f32[3,64,2,3072]{3,2,0,1:T(2,128)}, u32[]{:S(2)}, u32[]{:S(2)}) async-start(f32[3,64,2,3072]{3,2,0,1:T(2,128)} %copy.12), calls=%async_computation.1 | async-start | bytes 9437184 | tf_op jit(solution)/shard_map/all_to_all | solution.py:61
  118.7 110.6 %copy-start.1 = (bf16[3,2,3072]{2,1,0:T(2,128)(2,1)S(1)}, bf16[3,2,3072]{2,1,0:T(2,128)(2,1)}, u32[]{:S(2)}) copy-start(bf16[3,2,3072]{2,1,0:T(2,128)(2,1)} %param.15) | copy-start | bytes 110596
  118.7 115.6 %copy-start.2 = (f32[1,3072]{1,0:T(1,128)S(1)}, f32[1,3072]{1,0:T(1,128)}, u32[]{:S(2)}) copy-start(f32[1,3072]{1,0:T(1,128)} %param.16) | copy-start | bytes 36868
  229.4 4.7 collective-permute-start
  237.0 63.8 %all-to-all-start.2 = ((bf16[64,3,2,3072]{3,2,1,0:T(2,128)(2,1)}), bf16[64,3,2,3072]{3,2,1,0:T(2,128)(2,1)}, u32[]{:S(2)}, u32[]{:S(2)}) async-start(bf16[64,3,2,3072]{3,2,1,0:T(2,128)(2,1)} %stack.9), calls=%async_computation.2 | async-start | bytes 4718592 | tf_op jit(solution)/shard_map/all_to_all | solution.py:50
  455.7 4.7 collective-permute-start.1
  463.3 64.2 %all-to-all-start.4 = ((bf16[64,3,2,3072]{3,2,1,0:T(2,128)(2,1)}), bf16[64,3,2,3072]{3,2,1,0:T(2,128)(2,1)}, u32[]{:S(2)}, u32[]{:S(2)}) async-start(bf16[64,3,2,3072]{3,2,1,0:T(2,128)(2,1)} %stack.10), calls=%async_computation.4 | async-start | bytes 4718592 | tf_op jit(solution)/shard_map/all_to_all | solution.py:50
  682.8 70.4 %copy-start.3 = (bf16[3,2,3072]{2,1,0:T(2,128)(2,1)}, bf16[3,2,3072]{2,1,0:T(2,128)(2,1)S(1)}, u32[]{:S(2)}) copy-start(bf16[3,2,3072]{2,1,0:T(2,128)(2,1)S(1)} %fusion.87) | copy-start | bytes 110596
  682.8 4.7 collective-permute-start.2
  784.9 120.4 %all-to-all-start.7 = ((f32[3,64,2,3072]{3,2,0,1:T(2,128)}), f32[3,64,2,3072]{3,2,0,1:T(2,128)}, u32[]{:S(2)}, u32[]{:S(2)}) async-start(f32[3,64,2,3072]{3,2,0,1:T(2,128)} %copy.18), calls=%async_computation.7 | async-start | bytes 9437184 | tf_op jit(solution)/shard_map/all_to_all | solution.py:61
  798.1 110.8 %copy-start.4 = (bf16[3,2,3072]{2,1,0:T(2,128)(2,1)S(1)}, bf16[3,2,3072]{2,1,0:T(2,128)(2,1)}, u32[]{:S(2)}) copy-start(bf16[3,2,3072]{2,1,0:T(2,128)(2,1)} %copy-done.3) | copy-start | bytes 110596
